TPU v7x, 128 devices: a whole 4x4x4 slice. The times are simulated.
128 devices in a mesh: row: 8 (over x, core), col: 16 (over z, y).
Axes of the slice: x: 4, y: 4, z: 4, core: 2. Of those that a mesh axis runs over, the one named last changes fastest.
Arguments:
- features: float32 [32768, 128], P('col', 'row'), may hold values from -6 to 6
- tile_rows: int32 [8, 16, 80], P('row', 'col'), may hold values from 0 to 32, as said below
- tile_cols: int32 [8, 16, 80], P('row', 'col'), may hold values from 0 to 15
- tile_values: float32 [8, 16, 80, 128, 128], P('row', 'col'), may hold values from -0.51881118 to 0.51881118, as said below
- weight_in: float32 [128, 256], replicated, may hold values from -0.5 to 0.5
- weight_out: float32 [256, 256], replicated, may hold values from -0.375 to 0.375
- cotangent: float32 [32768, 256], P(('col', 'row')), may hold values from -0.03125 to 0.03125
Outputs:
- output: float32 [32768, 256], P(('col', 'row'))
- grad_in: float32 [128, 256], replicated
- grad_out: float32 [256, 256], replicated
Inputs may be any that keep to these rules, and one draw needn't show every extreme that they name: `tile_rows`: slot s of device (i, j) is used for s below that device's tile count and holds a tile row 0 to 31; unused slots hold 32. Used slots come first, no (row, column) pair repeats within a device, and in every draw some device uses all 80 slots. `tile_values`: A tile is sparse: each entry is nonzero with probability 2.56 / 128, at random positions.
All inputs are finite; a program needn't handle non-finite values.
Results may differ from a plain program's by a relative error of at most 0.0003.
Values sent between devices are 32-bit elements; how exact they have to be, the bound alone decides.
A program may use at most 128 MiB of HBM per device.

v0:
```python
import jax
import jax.numpy as jnp
from jax import lax
from jax.sharding import PartitionSpec as P

TILE = 128


def forward_tiles(gathered, tile_row, tile_col, tile_block, out_tiles):
    width = gathered.shape[1]
    blocks = gathered.reshape(-1, TILE, width)
    picked = jnp.take(blocks, tile_col, axis=0)
    products = jnp.einsum("tab,tbf->taf", tile_block, picked, precision=lax.Precision.HIGHEST)
    onehot = (tile_row[None, :] == jnp.arange(out_tiles, dtype=jnp.int32)[:, None]).astype(
        jnp.float32
    )
    summed = jnp.einsum("rt,taf->raf", onehot, products, precision=lax.Precision.HIGHEST)
    return summed.reshape(out_tiles * TILE, width)


def adjoint_tiles(row_grads, tile_row, tile_col, tile_block, out_tiles):
    width = row_grads.shape[1]
    in_tiles = row_grads.shape[0] // TILE
    blocks = row_grads.reshape(in_tiles, TILE, width)
    picked = jnp.take(blocks, jnp.minimum(tile_row, in_tiles - 1), axis=0)
    products = jnp.einsum("tba,tbf->taf", tile_block, picked, precision=lax.Precision.HIGHEST)
    matches = tile_col[None, :] == jnp.arange(out_tiles, dtype=jnp.int32)[:, None]
    onehot = (matches & (tile_row < in_tiles)[None, :]).astype(jnp.float32)
    summed = jnp.einsum("rt,taf->raf", onehot, products, precision=lax.Precision.HIGHEST)
    return summed.reshape(out_tiles * TILE, width)


def dense_product(left, right):
    return jnp.dot(left, right, precision=lax.Precision.HIGHEST, preferred_element_type=jnp.float32)


def inner_rows(left, right):
    return lax.dot_general(
        left,
        right,
        (((0,), (0,)), ((), ())),
        precision=lax.Precision.HIGHEST,
        preferred_element_type=jnp.float32,
    )


def per_device(features, tile_rows, tile_cols, tile_values, weight_in, weight_out, cotangent):
    tile_row = tile_rows.reshape(-1)
    tile_col = tile_cols.reshape(-1)
    tile_block = tile_values.reshape(-1, TILE, TILE)
    local_rows = cotangent.shape[0]
    row_tiles = lax.axis_size("col") * local_rows // TILE
    col_tiles = lax.axis_size("row") * local_rows // TILE
    x_local = lax.all_to_all(features, "row", split_axis=0, concat_axis=1, tiled=True)
    support = dense_product(x_local, weight_in)
    gathered = lax.all_gather(support, "row", axis=0, tiled=True)
    partial_one = forward_tiles(gathered, tile_row, tile_col, tile_block, row_tiles)
    pre_act = lax.psum_scatter(partial_one, "col", scatter_dimension=0, tiled=True)
    hidden = jax.nn.silu(pre_act)
    support_two = dense_product(hidden, weight_out)
    gathered_two = lax.all_gather(support_two, "row", axis=0, tiled=True)
    partial_two = forward_tiles(gathered_two, tile_row, tile_col, tile_block, row_tiles)
    output = lax.psum_scatter(partial_two, "col", scatter_dimension=0, tiled=True)
    rows_out = lax.all_gather(cotangent, "col", axis=0, tiled=True)
    adjoint_two = adjoint_tiles(rows_out, tile_row, tile_col, tile_block, col_tiles)
    d_support_two = lax.psum_scatter(adjoint_two, "row", scatter_dimension=0, tiled=True)
    grad_out_local = inner_rows(hidden, d_support_two)
    d_hidden = dense_product(d_support_two, weight_out.T)
    sigmoid_pre = jax.nn.sigmoid(pre_act)
    d_pre = d_hidden * sigmoid_pre * (1.0 + pre_act * (1.0 - sigmoid_pre))
    rows_in = lax.all_gather(d_pre, "col", axis=0, tiled=True)
    adjoint_one = adjoint_tiles(rows_in, tile_row, tile_col, tile_block, col_tiles)
    d_support = lax.psum_scatter(adjoint_one, "row", scatter_dimension=0, tiled=True)
    grad_in_local = inner_rows(x_local, d_support)
    grad_in, grad_out = lax.psum((grad_in_local, grad_out_local), ("row", "col"))
    return (output, grad_in, grad_out)


def solution(mesh):
    return jax.shard_map(
        per_device,
        mesh=mesh,
        in_specs=(
            P("col", "row"),
            P("row", "col", None),
            P("row", "col", None),
            P("row", "col", None, None, None),
            P(),
            P(),
            P(("col", "row"), None),
        ),
        out_specs=(P(("col", "row"), None), P(), P()),
        check_vma=False,
    )
```

profile of v0, /device:TPU:0, one launch (start us, length us, event | category | flops | bytes accessed | tf_op | source)
XLA Modules:
  0.0 643.5 jit_solution(13298213714380566996)
XLA Ops:
  7.2 0.0 copy-start
  7.2 0.0 all-gather.9.cloned.1.call-start
  7.2 0.7 all-gather.9.cloned.1.call-update
  7.9 0.0 all-gather.5.cloned.1.call-start
  8.0 0.9 copy.60
  8.9 10.3 %all_to_all.19 = f32[8,256,16]{1,2,0:T(8,128)S(1)} all-to-all(f32[8,256,16]{1,2,0:T(8,128)S(1)} %bitcast.80), channel_id=1, replica_groups=mesh['row'=8,'col'=16] {'row'}, dimensions={0} | all-to-all | bytes 262144 | tf_op jit(solution)/shard_map/all_to_all | solution.py:54
  19.2 2.0 fusion.69
  21.2 0.0 all-gather.5.cloned.1.call-update
  21.2 0.0 reduce-scatter.9.cloned.1.call-start
  21.3 0.7 compare_and_fusion
  22.0 42.2 %all-gather.9.cloned.1.call-done = f32[4096,256]{1,0:T(8,128)} async-done(((f32[256,256]{1,0:T(8,128)}), f32[4096,256]{1,0:T(8,128)}) %all-gather.9.cloned.1.call-update) | async-done | bytes 4194320 | tf_op jit(solution)/shard_map/all_gather | solution.py:64
  64.2 9.9 %gather_fusion.2 = f32[80,128,256]{2,1,0:T(8,128)} fusion(f32[32,128,256]{2,1,0:T(8,128)} %bitcast.72, s32[1024]{0:T(1024)S(1)} %pad_clamp_fusion), kind=kCustom, calls=%fused_computation.1.clone | custom fusion | bytes 20971840 | tf_op jit(solution)/shard_map/jit(_take)/gather | solution.py:25
  74.0 23.1 %fusion.30 = f32[80,128,256]{1,2,0:T(8,128)} fusion(f32[1,1,80,128,128]{4,3,2,1,0:T(8,128)} %param.14, f32[80,128,256]{2,1,0:T(8,128)} %gather_fusion.2, pred[80]{0:T(512)(128)(4,1)S(1)} %get-tuple-element.22), kind=kOutput, calls=%fused_computation.26 | convolution fusion | flops 4029153280 | bytes 26214480 | tf_op jit(solution)/shard_map/tba,tbf->taf/dot_general | solution.py:26
  97.2 0.0 copy-start.3
  97.2 11.6 %copy.48 = f32[80,128,256]{2,0,1:T(8,128)} copy(f32[80,128,256]{1,2,0:T(8,128)} %fusion.30) | data formatting | bytes 20971520 | tf_op jit(solution)/shard_map/tba,tbf->taf/dot_general | solution.py:26
  108.8 0.0 copy-done.3
  108.8 6.2 fusion.57
  115.1 2.6 copy.49
  117.7 0.0 reduce-scatter.9.cloned.1.call-update
  117.7 0.4 reduce-scatter.5.cloned.1.call-start
  118.1 0.0 all-gather.5.cloned.1.call-done
  118.1 9.9 %gather_fusion = f32[80,128,256]{2,1,0:T(8,128)} fusion(f32[16,128,256]{2,1,0:T(8,128)} %bitcast.70, s32[1024]{0:T(1024)S(1)} %pad_clamp_fusion.1), kind=kCustom, calls=%fused_computation.clone | custom fusion | bytes 20971840 | tf_op jit(solution)/shard_map/jit(_take)/gather | solution.py:12
  128.0 23.0 %fusion.20 = f32[80,128,256]{1,2,0:T(8,128)} fusion(f32[1,1,80,128,128]{4,3,2,1,0:T(8,128)} %param.14, f32[80,128,256]{2,1,0:T(8,128)} %gather_fusion, pred[80]{0:T(512)(128)(4,1)S(1)} %compare_and_fusion.1), kind=kOutput, calls=%fused_computation.24 | convolution fusion | flops 4029153280 | bytes 26214480 | tf_op jit(solution)/shard_map/tab,tbf->taf/dot_general | solution.py:13
  151.0 11.7 %copy.42 = f32[80,128,256]{2,0,1:T(8,128)} copy(f32[80,128,256]{1,2,0:T(8,128)} %fusion.20) | data formatting | bytes 20971520 | tf_op jit(solution)/shard_map/tab,tbf->taf/dot_general | solution.py:13
  162.7 0.0 copy-done.2
  162.7 6.9 %fusion.49 = f32[32,128,256]{2,0,1:T(8,128)S(1)} fusion(f32[80,128,256]{2,0,1:T(8,128)} %copy.42, s32[80]{0:T(128)S(1)} %bitcast.82), kind=kOutput, calls=%fused_computation.39 | convolution fusion | flops 1006635520 | bytes 14680384 | tf_op jit(solution)/shard_map/rt,taf->raf/dot_general | solution.py:17
  169.6 4.4 copy.43
  173.9 0.0 reduce-scatter.5.cloned.1.call-update
  174.0 0.0 all-gather.11.cloned.1.call-start
  174.0 0.0 reduce-scatter.9.cloned.1.call-done
  174.0 78.6 %reduce-scatter.5.cloned.1.call-done = f32[256,256]{1,0:T(8,128)} async-done(((f32[4096,256]{1,0:T(8,128)}), f32[256,256]{1,0:T(8,128)}) %reduce-scatter.5.cloned.1.call-update) | async-done | bytes 262160 | tf_op jit(solution)/shard_map/reduce_scatter | solution.py:58
  252.6 0.0 copy-done
  252.6 2.1 fusion.40
  254.7 0.0 all-gather.11.cloned.1.call-update
  254.8 0.0 all-gather.7.cloned.1.call-start
  254.8 2.1 fusion.44
  256.9 0.0 all-gather.7.cloned.1.call-update
  256.9 0.0 reduce-scatter.11.cloned.1.call-start
  257.0 48.8 %all-gather.11.cloned.1.call-done = f32[4096,256]{1,0:T(8,128)} async-done(((f32[256,256]{1,0:T(8,128)}), f32[4096,256]{1,0:T(8,128)}) %all-gather.11.cloned.1.call-update) | async-done | bytes 4194320 | tf_op jit(solution)/shard_map/all_gather | solution.py:71
  305.8 10.1 %gather_fusion.3 = f32[80,128,256]{2,1,0:T(8,128)} fusion(f32[32,128,256]{2,1,0:T(8,128)} %bitcast.73, s32[1024]{0:T(1024)S(1)} %pad_clamp_fusion), kind=kCustom, calls=%fused_computation.3.clone | custom fusion | bytes 20971840 | tf_op jit(solution)/shard_map/jit(_take)/gather | solution.py:25
  315.8 23.2 %fusion.35 = f32[80,128,256]{1,2,0:T(8,128)} fusion(f32[1,1,80,128,128]{4,3,2,1,0:T(8,128)} %param.14, f32[80,128,256]{2,1,0:T(8,128)} %gather_fusion.3, pred[80]{0:T(512)(128)(4,1)S(1)} %get-tuple-element.22), kind=kOutput, calls=%fused_computation.27 | convolution fusion | flops 4029153280 | bytes 26214480 | tf_op jit(solution)/shard_map/tba,tbf->taf/dot_general | solution.py:26
  339.1 11.6 %copy.51 = f32[80,128,256]{2,0,1:T(8,128)} copy(f32[80,128,256]{1,2,0:T(8,128)} %fusion.35) | data formatting | bytes 20971520 | tf_op jit(solution)/shard_map/tba,tbf->taf/dot_general | solution.py:26
  350.7 6.3 fusion.55
  357.0 2.6 copy.52
  359.6 0.0 reduce-scatter.11.cloned.1.call-update
  359.6 0.3 all-reduce.3.cloned.1.call-start
  359.9 0.0 copy-done.4
  359.9 0.0 copy-done.5
  359.9 1.3 fusion.42
  361.2 9.8 %gather_fusion.1 = f32[80,128,256]{2,1,0:T(8,128)} fusion(f32[16,128,256]{2,1,0:T(8,128)} %bitcast.71, s32[1024]{0:T(1024)S(1)} %pad_clamp_fusion.1), kind=kCustom, calls=%fused_computation.2.clone | custom fusion | bytes 20971840 | tf_op jit(solution)/shard_map/jit(_take)/gather | solution.py:12
  371.0 23.0 %fusion.25 = f32[80,128,256]{1,2,0:T(8,128)} fusion(f32[1,1,80,128,128]{4,3,2,1,0:T(8,128)} %param.14, f32[80,128,256]{2,1,0:T(8,128)} %gather_fusion.1, pred[80]{0:T(512)(128)(4,1)S(1)} %compare_and_fusion.1), kind=kOutput, calls=%fused_computation.25 | convolution fusion | flops 4029153280 | bytes 26214480 | tf_op jit(solution)/shard_map/tab,tbf->taf/dot_general | solution.py:13
  394.0 11.6 %copy.45 = f32[80,128,256]{2,0,1:T(8,128)} copy(f32[80,128,256]{1,2,0:T(8,128)} %fusion.25) | data formatting | bytes 20971520 | tf_op jit(solution)/shard_map/tab,tbf->taf/dot_general | solution.py:13
  405.6 2.2 convolution_bitcast_fusion
  407.8 0.0 all-reduce.3.cloned.1.call-update
  407.9 0.0 copy-start.1
  407.9 0.3 reduce-scatter.7.cloned.1.call-start
  408.2 6.9 %fusion.47 = f32[32,128,256]{2,0,1:T(8,128)S(1)} fusion(f32[80,128,256]{2,0,1:T(8,128)} %copy.45, s32[80]{0:T(128)S(1)} %bitcast.83), kind=kOutput, calls=%fused_computation.38 | convolution fusion | flops 1006635520 | bytes 14680384 | tf_op jit(solution)/shard_map/rt,taf->raf/dot_general | solution.py:17
  415.1 4.4 copy.46
  419.4 0.0 reduce-scatter.7.cloned.1.call-update
  419.4 134.7 %all-reduce.3.cloned.1.call-done = (f32[128,256]{0,1:T(8,128)}, f32[256,256]{1,0:T(8,128)}) async-done(((f32[128,256]{0,1:T(8,128)}, f32[256,256]{1,0:T(8,128)}), (f32[128,256]{0,1:T(8,128)}, f32[256,256]{1,0:T(8,128)})) %all-reduce.3.cloned.1.call-update) | async-done | bytes 393232 | tf_op jit(solution)/shard_map/psum | solution.py:75
  554.2 1.7 copy.53
  555.8 79.0 %reduce-scatter.7.cloned.1.call-done = f32[256,256]{1,0:T(8,128)} async-done(((f32[4096,256]{1,0:T(8,128)}), f32[256,256]{1,0:T(8,128)}) %reduce-scatter.7.cloned.1.call-update) | async-done | bytes 262160 | tf_op jit(solution)/shard_map/reduce_scatter | solution.py:63
  634.9 1.7 copy.63
  636.5 0.0 copy-done.1
  (9 shorter events, 0.0 us)
Async XLA Ops:
  7.2 245.4 %copy-start = (f32[256,256]{1,0:T(8,128)S(1)}, f32[256,256]{1,0:T(8,128)}, u32[]{:S(2)}) copy-start(f32[256,256]{1,0:T(8,128)} %param.16) | copy-start | bytes 786436
  7.2 57.0 %all-gather.9.cloned.1.call-start = ((), (), s32[]{:S(2)}) async-start(), calls=%async_computation.9 | async-start | bytes 4456448 | tf_op jit(solution)/shard_map/all_gather | solution.py:64
  7.9 110.2 %all-gather.5.cloned.1.call-start = ((), (), s32[]{:S(2)}) async-start(), calls=%async_computation.5 | async-start | bytes 2359296 | tf_op jit(solution)/shard_map/all_gather | solution.py:56
  21.2 152.8 %reduce-scatter.9.cloned.1.call-start = ((), (), s32[]{:S(2)}) async-start(), calls=%async_computation.10 | async-start | bytes 2359296 | tf_op jit(solution)/shard_map/reduce_scatter | solution.py:66
  97.2 11.7 %copy-start.3 = (s32[1,1,80]{2,1,0:T(1,128)S(1)}, s32[1,1,80]{2,1,0:T(1,128)}, u32[]{:S(2)}) copy-start(s32[1,1,80]{2,1,0:T(1,128)} %param.13) | copy-start | bytes 964
  117.7 134.9 %reduce-scatter.5.cloned.1.call-start = ((), (), s32[]{:S(2)}) async-start(), calls=%async_computation.6 | async-start | bytes 4456448 | tf_op jit(solution)/shard_map/reduce_scatter | solution.py:58
  151.0 11.7 %copy-start.2 = (s32[1,1,80]{2,1,0:T(1,128)S(1)}, s32[1,1,80]{2,1,0:T(1,128)}, u32[]{:S(2)}) copy-start(s32[1,1,80]{2,1,0:T(1,128)} %param.12) | copy-start | bytes 964
  174.0 131.8 %all-gather.11.cloned.1.call-start = ((), (), s32[]{:S(2)}) async-start(), calls=%async_computation.11 | async-start | bytes 4456448 | tf_op jit(solution)/shard_map/all_gather | solution.py:71
  254.8 106.4 %all-gather.7.cloned.1.call-start = ((), (), s32[]{:S(2)}) async-start(), calls=%async_computation.7 | async-start | bytes 2359296 | tf_op jit(solution)/shard_map/all_gather | solution.py:61
  256.9 148.7 %reduce-scatter.11.cloned.1.call-start = ((), (), s32[]{:S(2)}) async-start(), calls=%async_computation.12 | async-start | bytes 2359296 | tf_op jit(solution)/shard_map/reduce_scatter | solution.py:73
  350.7 9.2 %copy-start.4 = (f32[256,256]{1,0:T(8,128)S(1)}, f32[256,256]{1,0:T(8,128)}, u32[]{:S(2)}) copy-start(f32[256,256]{1,0:T(8,128)} %reduce-scatter.9.cloned.1.call-done) | copy-start | bytes 786436
  350.7 9.2 %copy-start.5 = (f32[256,256]{1,0:T(8,128)S(1)}, f32[256,256]{1,0:T(8,128)}, u32[]{:S(2)}) copy-start(f32[256,256]{1,0:T(8,128)} %reduce-scatter.5.cloned.1.call-done) | copy-start | bytes 786436
  359.6 194.6 %all-reduce.3.cloned.1.call-start = ((), (), s32[]{:S(2)}) async-start(), calls=%async_computation.13 | async-start | bytes 786432 | tf_op jit(solution)/shard_map/psum | solution.py:75
  407.9 228.7 %copy-start.1 = (f32[256,256]{1,0:T(8,128)S(1)}, f32[256,256]{1,0:T(8,128)}, u32[]{:S(2)}) copy-start(f32[256,256]{1,0:T(8,128)} %param.16) | copy-start | bytes 786436
  407.9 227.0 %reduce-scatter.7.cloned.1.call-start = ((), (), s32[]{:S(2)}) async-start(), calls=%async_computation.8 | async-start | bytes 4456448 | tf_op jit(solution)/shard_map/reduce_scatter | solution.py:63
Sparse Core Ops, SparseCore 0:
  10.1 53.9 all-gather.8
  66.5 24.8 all-gather.4
  117.8 33.6 reduce-scatter.8
  174.1 78.4 reduce-scatter.4
  255.1 50.5 all-gather.10
  307.9 24.8 all-gather.6
  359.7 33.6 reduce-scatter.10
  408.0 146.1 all-reduce.2
  558.1 76.7 reduce-scatter.6
where the time goes:
time: 653 us; the launch traced here: 644 us
  waiting for transfers between devices  384 us (59%)
  matrix products  128 us (20%)
  local copies, waits for them, and re-layouts  104 us (16%)
  between operations  14.4 us (2%)
  blocking collectives  10.3 us (2%)
    psum x1, waiting for transfers between devices, per_device(): lax.psum((grad_in_local, grad_out_local), ('row', 'col'))  135 us
    reduce_scatter x1, waiting for transfers between devices, per_device(): lax.psum_scatter(partial_two, 'col', scatter_dimension=0, tiled=True)  79 us
    reduce_scatter x1, waiting for transfers between devices, per_device(): lax.psum_scatter(partial_one, 'col', scatter_dimension=0, tiled=True)  78.6 us
    all_gather x1, waiting for transfers between devices, per_device(): rows_in = lax.all_gather(d_pre, 'col', axis=0, tiled=True)  48.8 us
    dot_general x2, matrix products, adjoint_tiles(): jnp.einsum('tba,tbf->taf', tile_block, picked, precision=lax.Precision.HI...  46.4 us
    dot_general x2, matrix products, forward_tiles(): jnp.einsum('tab,tbf->taf', tile_block, picked, precision=lax.Precision.HI...  46 us
    all_gather x1, waiting for transfers between devices, per_device(): rows_out = lax.all_gather(cotangent, 'col', axis=0, tiled=True)  42.2 us
    dot_general x2, local copies, waits for them, and re-layouts, forward_tiles(): jnp.einsum('tab,tbf->taf', tile_block, picked, precision=lax.Precision.HI...  23.3 us
  transfers between devices with their start and end apart: 9, of which 5 were waited for; matrix products, arithmetic and copies ran while one was open for 35% of the time, Pallas kernels for 0%

commit v1 on v0

--- a/solution.py
+++ b/solution.py
@@ -61,7 +61,13 @@
     gathered_two = lax.all_gather(support_two, "row", axis=0, tiled=True)
     partial_two = forward_tiles(gathered_two, tile_row, tile_col, tile_block, row_tiles)
     output = lax.psum_scatter(partial_two, "col", scatter_dimension=0, tiled=True)
-    rows_out = lax.all_gather(cotangent, "col", axis=0, tiled=True)
+
+    def samples_tell(inp, which_axis):
+        return jnp.concatenate(
+            lax.all_to_all(jnp.stack(lax.axis_size(which_axis) * [inp]), which_axis, 0, 0), axis=0
+        )
+
+    rows_out = samples_tell(cotangent, which_axis="col")
     adjoint_two = adjoint_tiles(rows_out, tile_row, tile_col, tile_block, col_tiles)
     d_support_two = lax.psum_scatter(adjoint_two, "row", scatter_dimension=0, tiled=True)
     grad_out_local = inner_rows(hidden, d_support_two)

time: 653 us -> 680 us (1.041)
  waiting for transfers between devices: 384 us -> 401 us
  starting transfers between devices: 1.18 us -> 9.24 us
    all_to_all x0 -> x1, waiting for transfers between devices: none -> 61.6 us  [samples_tell(): lax.all_to_all(jnp.stack(lax.axis_size(which_axis) * [inp]), which_axis,...]
    all_gather x1 -> x0, waiting for transfers between devices: 42.2 us -> none  [per_device(): rows_out = lax.all_gather(cotangent, 'col', axis=0, tiled=True)]
    all_to_all x0 -> x1, starting transfers between devices: none -> 8.1 us  [samples_tell(): lax.all_to_all(jnp.stack(lax.axis_size(which_axis) * [inp]), which_axis,...]
  transfers between devices with their start and end apart: 9 -> 9, of which waited for: 5 -> 5; matrix products, arithmetic and copies ran while one was open for 35% -> 34% of each run, Pallas kernels for 0% -> 0%
where the time goes in v1:
time: 680 us; the launch traced here: 670 us
  waiting for transfers between devices  401 us (59%)
  matrix products  127 us (19%)
  local copies, waits for them, and re-layouts  108 us (16%)
  between operations  14.7 us (2%)
  blocking collectives  10.3 us (2%)
  starting transfers between devices  9.24 us (1%)
    psum x1, waiting for transfers between devices, per_device(): lax.psum((grad_in_local, grad_out_local), ('row', 'col'))  135 us
    reduce_scatter x1, waiting for transfers between devices, per_device(): lax.psum_scatter(partial_two, 'col', scatter_dimension=0, tiled=True)  79 us
    reduce_scatter x1, waiting for transfers between devices, per_device(): lax.psum_scatter(partial_one, 'col', scatter_dimension=0, tiled=True)  76.5 us
    all_to_all x1, waiting for transfers between devices, samples_tell(): lax.all_to_all(jnp.stack(lax.axis_size(which_axis) * [inp]), which_axis,...  61.6 us
    all_gather x1, waiting for transfers between devices, per_device(): rows_in = lax.all_gather(d_pre, 'col', axis=0, tiled=True)  48.8 us
    dot_general x2, matrix products, adjoint_tiles(): jnp.einsum('tba,tbf->taf', tile_block, picked, precision=lax.Precision.HI...  46.1 us
    dot_general x2, matrix products, forward_tiles(): jnp.einsum('tab,tbf->taf', tile_block, picked, precision=lax.Precision.HI...  46.1 us
    dot_general x2, local copies, waits for them, and re-layouts, adjoint_tiles(): jnp.einsum('tba,tbf->taf', tile_block, picked, precision=lax.Precision.HI...  23.3 us
  transfers between devices with their start and end apart: 9, of which 5 were waited for; matrix products, arithmetic and copies ran while one was open for 34% of the time, Pallas kernels for 0%

profile of v1, /device:TPU:0, one launch (start us, length us, event | category | flops | bytes accessed | tf_op | source)
XLA Modules:
  0.0 670.0 jit_solution(15980502739268783157)
XLA Ops:
  7.2 0.0 copy-start
  7.2 0.0 copy-start.2
  7.2 0.0 copy-start.3
  7.2 1.0 copy.60
  8.2 10.3 %all_to_all.24 = f32[8,256,16]{1,2,0:T(8,128)S(1)} all-to-all(f32[8,256,16]{1,2,0:T(8,128)S(1)} %bitcast.79), channel_id=1, replica_groups=mesh['row'=8,'col'=16] {'row'}, dimensions={0} | all-to-all | bytes 262144 | tf_op jit(solution)/shard_map/all_to_all | solution.py:54
  18.5 3.3 stack.2
  21.8 8.1 %all-to-all-start.1 = ((f32[16,256,256]{2,1,0:T(8,128)}), f32[16,256,256]{2,1,0:T(8,128)}, u32[]{:S(2)}, u32[]{:S(2)}) async-start(f32[16,256,256]{2,1,0:T(8,128)} %stack.2), calls=%async_computation.3 | async-start | bytes 8388608 | tf_op jit(solution)/shard_map/all_to_all | solution.py:67
  29.9 0.0 all-gather.4.cloned.1.call-start
  29.9 0.0 copy-done.2
  29.9 1.1 fusion.69
  31.1 0.0 all-gather.4.cloned.1.call-update
  31.1 0.0 reduce-scatter.9.cloned.1.call-start
  31.1 0.0 copy-done.3
  31.2 61.6 %all-to-all-done.1 = f32[16,256,256]{2,1,0:T(8,128)} async-done(((f32[16,256,256]{2,1,0:T(8,128)}), f32[16,256,256]{2,1,0:T(8,128)}, u32[]{:S(2)}, u32[]{:S(2)}) %all-to-all-start.1) | async-done | bytes 4194336 | tf_op jit(solution)/shard_map/all_to_all | solution.py:67
  92.8 9.9 %gather_fusion.2 = f32[80,128,256]{2,1,0:T(8,128)} fusion(f32[32,128,256]{2,1,0:T(8,128)} %bitcast.13, s32[1024]{0:T(1024)S(1)} %pad_clamp_fusion), kind=kCustom, calls=%fused_computation.1.clone | custom fusion | bytes 20971840 | tf_op jit(solution)/shard_map/jit(_take)/gather | solution.py:25
  102.6 22.9 %fusion.30 = f32[80,128,256]{1,2,0:T(8,128)} fusion(f32[1,1,80,128,128]{4,3,2,1,0:T(8,128)} %param.14, f32[80,128,256]{2,1,0:T(8,128)} %gather_fusion.2, pred[80]{0:T(512)(128)(4,1)S(1)} %get-tuple-element.22), kind=kOutput, calls=%fused_computation.26 | convolution fusion | flops 4029153280 | bytes 26214480 | tf_op jit(solution)/shard_map/tba,tbf->taf/dot_general | solution.py:26
  125.6 11.6 %copy.48 = f32[80,128,256]{2,0,1:T(8,128)} copy(f32[80,128,256]{1,2,0:T(8,128)} %fusion.30) | data formatting | bytes 20971520 | tf_op jit(solution)/shard_map/tba,tbf->taf/dot_general | solution.py:26
  137.2 0.0 copy-done.4
  137.2 6.2 fusion.57
  143.4 2.6 copy.49
  146.0 0.0 reduce-scatter.9.cloned.1.call-update
  146.1 0.4 reduce-scatter.5.cloned.1.call-start
  146.5 0.0 all-gather.4.cloned.1.call-done
  146.5 9.7 %gather_fusion = f32[80,128,256]{2,1,0:T(8,128)} fusion(f32[16,128,256]{2,1,0:T(8,128)} %bitcast.70, s32[1024]{0:T(1024)S(1)} %pad_clamp_fusion.1), kind=kCustom, calls=%fused_computation.clone | custom fusion | bytes 20971840 | tf_op jit(solution)/shard_map/jit(_take)/gather | solution.py:12
  156.2 23.1 %fusion.20 = f32[80,128,256]{1,2,0:T(8,128)} fusion(f32[1,1,80,128,128]{4,3,2,1,0:T(8,128)} %param.14, f32[80,128,256]{2,1,0:T(8,128)} %gather_fusion, pred[80]{0:T(512)(128)(4,1)S(1)} %compare_and_fusion.1), kind=kOutput, calls=%fused_computation.24 | convolution fusion | flops 4029153280 | bytes 26214480 | tf_op jit(solution)/shard_map/tab,tbf->taf/dot_general | solution.py:13
  179.3 11.6 %copy.42 = f32[80,128,256]{2,0,1:T(8,128)} copy(f32[80,128,256]{1,2,0:T(8,128)} %fusion.20) | data formatting | bytes 20971520 | tf_op jit(solution)/shard_map/tab,tbf->taf/dot_general | solution.py:13
  191.0 6.9 %fusion.49 = f32[32,128,256]{2,0,1:T(8,128)S(1)} fusion(f32[80,128,256]{2,0,1:T(8,128)} %copy.42, s32[80]{0:T(128)S(1)} %bitcast.81), kind=kOutput, calls=%fused_computation.39 | convolution fusion | flops 1006635520 | bytes 14680384 | tf_op jit(solution)/shard_map/rt,taf->raf/dot_general | solution.py:17
  197.8 4.4 copy.43
  202.2 0.0 reduce-scatter.5.cloned.1.call-update
  202.2 0.0 all-gather.8.cloned.1.call-start
  202.3 0.0 reduce-scatter.9.cloned.1.call-done
  202.3 76.5 %reduce-scatter.5.cloned.1.call-done = f32[256,256]{1,0:T(8,128)} async-done(((f32[4096,256]{1,0:T(8,128)}), f32[256,256]{1,0:T(8,128)}) %reduce-scatter.5.cloned.1.call-update) | async-done | bytes 262160 | tf_op jit(solution)/shard_map/reduce_scatter | solution.py:58
  278.8 0.0 copy-done
  278.8 2.1 fusion.40
  280.9 0.0 all-gather.8.cloned.1.call-update
  280.9 0.0 all-gather.6.cloned.1.call-start
  281.0 2.1 fusion.44
  283.1 0.0 all-gather.6.cloned.1.call-update
  283.1 0.0 reduce-scatter.11.cloned.1.call-start
  283.1 48.8 %all-gather.8.cloned.1.call-done = f32[4096,256]{1,0:T(8,128)} async-done(((f32[256,256]{1,0:T(8,128)}), f32[4096,256]{1,0:T(8,128)}) %all-gather.8.cloned.1.call-update) | async-done | bytes 4194320 | tf_op jit(solution)/shard_map/all_gather | solution.py:77
  332.0 10.1 %gather_fusion.3 = f32[80,128,256]{2,1,0:T(8,128)} fusion(f32[32,128,256]{2,1,0:T(8,128)} %bitcast.72, s32[1024]{0:T(1024)S(1)} %pad_clamp_fusion), kind=kCustom, calls=%fused_computation.3.clone | custom fusion | bytes 20971840 | tf_op jit(solution)/shard_map/jit(_take)/gather | solution.py:25
  342.0 23.2 %fusion.35 = f32[80,128,256]{1,2,0:T(8,128)} fusion(f32[1,1,80,128,128]{4,3,2,1,0:T(8,128)} %param.14, f32[80,128,256]{2,1,0:T(8,128)} %gather_fusion.3, pred[80]{0:T(512)(128)(4,1)S(1)} %get-tuple-element.22), kind=kOutput, calls=%fused_computation.27 | convolution fusion | flops 4029153280 | bytes 26214480 | tf_op jit(solution)/shard_map/tba,tbf->taf/dot_general | solution.py:26
  365.2 11.6 %copy.51 = f32[80,128,256]{2,0,1:T(8,128)} copy(f32[80,128,256]{1,2,0:T(8,128)} %fusion.35) | data formatting | bytes 20971520 | tf_op jit(solution)/shard_map/tba,tbf->taf/dot_general | solution.py:26
  376.9 6.3 fusion.55
  383.2 2.6 copy.52
  385.7 0.0 reduce-scatter.11.cloned.1.call-update
  385.8 0.3 all-reduce.3.cloned.1.call-start
  386.0 0.0 copy-done.5
  386.0 0.0 copy-done.6
  386.1 1.3 fusion.42
  387.4 9.8 %gather_fusion.1 = f32[80,128,256]{2,1,0:T(8,128)} fusion(f32[16,128,256]{2,1,0:T(8,128)} %bitcast.71, s32[1024]{0:T(1024)S(1)} %pad_clamp_fusion.1), kind=kCustom, calls=%fused_computation.2.clone | custom fusion | bytes 20971840 | tf_op jit(solution)/shard_map/jit(_take)/gather | solution.py:12
  397.2 23.0 %fusion.25 = f32[80,128,256]{1,2,0:T(8,128)} fusion(f32[1,1,80,128,128]{4,3,2,1,0:T(8,128)} %param.14, f32[80,128,256]{2,1,0:T(8,128)} %gather_fusion.1, pred[80]{0:T(512)(128)(4,1)S(1)} %compare_and_fusion.1), kind=kOutput, calls=%fused_computation.25 | convolution fusion | flops 4029153280 | bytes 26214480 | tf_op jit(solution)/shard_map/tab,tbf->taf/dot_general | solution.py:13
  420.2 11.6 %copy.45 = f32[80,128,256]{2,0,1:T(8,128)} copy(f32[80,128,256]{1,2,0:T(8,128)} %fusion.25) | data formatting | bytes 20971520 | tf_op jit(solution)/shard_map/tab,tbf->taf/dot_general | solution.py:13
  431.8 2.2 convolution_bitcast_fusion
  434.0 0.0 all-reduce.3.cloned.1.call-update
  434.0 0.0 copy-start.1
  434.1 0.3 reduce-scatter.7.cloned.1.call-start
  434.4 6.9 %fusion.47 = f32[32,128,256]{2,0,1:T(8,128)S(1)} fusion(f32[80,128,256]{2,0,1:T(8,128)} %copy.45, s32[80]{0:T(128)S(1)} %bitcast.82), kind=kOutput, calls=%fused_computation.38 | convolution fusion | flops 1006635520 | bytes 14680384 | tf_op jit(solution)/shard_map/rt,taf->raf/dot_general | solution.py:17
  441.2 4.4 copy.46
  445.6 0.0 reduce-scatter.7.cloned.1.call-update
  445.6 134.7 %all-reduce.3.cloned.1.call-done = (f32[128,256]{0,1:T(8,128)}, f32[256,256]{1,0:T(8,128)}) async-done(((f32[128,256]{0,1:T(8,128)}, f32[256,256]{1,0:T(8,128)}), (f32[128,256]{0,1:T(8,128)}, f32[256,256]{1,0:T(8,128)})) %all-reduce.3.cloned.1.call-update) | async-done | bytes 393232 | tf_op jit(solution)/shard_map/psum | solution.py:81
  580.3 1.7 copy.53
  582.0 79.0 %reduce-scatter.7.cloned.1.call-done = f32[256,256]{1,0:T(8,128)} async-done(((f32[4096,256]{1,0:T(8,128)}), f32[256,256]{1,0:T(8,128)}) %reduce-scatter.7.cloned.1.call-update) | async-done | bytes 262160 | tf_op jit(solution)/shard_map/reduce_scatter | solution.py:63
  661.1 1.7 copy.63
  (11 shorter events, 0.0 us)
Async XLA Ops:
  7.2 271.6 %copy-start = (f32[256,256]{1,0:T(8,128)S(1)}, f32[256,256]{1,0:T(8,128)}, u32[]{:S(2)}) copy-start(f32[256,256]{1,0:T(8,128)} %param.16) | copy-start | bytes 786436
  7.2 22.8 %copy-start.2 = (f32[128,256]{1,0:T(8,128)S(1)}, f32[128,256]{1,0:T(8,128)}, u32[]{:S(2)}) copy-start(f32[128,256]{1,0:T(8,128)} %param.15) | copy-start | bytes 393220
  7.2 23.9 %copy-start.3 = (s32[1,1,80]{2,1,0:T(1,128)S(1)}, s32[1,1,80]{2,1,0:T(1,128)}, u32[]{:S(2)}) copy-start(s32[1,1,80]{2,1,0:T(1,128)} %param.12) | copy-start | bytes 964
  21.8 71.0 %all-to-all-start.1 = ((f32[16,256,256]{2,1,0:T(8,128)}), f32[16,256,256]{2,1,0:T(8,128)}, u32[]{:S(2)}, u32[]{:S(2)}) async-start(f32[16,256,256]{2,1,0:T(8,128)} %stack.2), calls=%async_computation.3 | async-start | bytes 8388608 | tf_op jit(solution)/shard_map/all_to_all | solution.py:67
  29.9 116.6 %all-gather.4.cloned.1.call-start = ((), (), s32[]{:S(2)}) async-start(), calls=%async_computation.6 | async-start | bytes 2359296 | tf_op jit(solution)/shard_map/all_gather | solution.py:56
  31.1 171.2 %reduce-scatter.9.cloned.1.call-start = ((), (), s32[]{:S(2)}) async-start(), calls=%async_computation.10 | async-start | bytes 2359296 | tf_op jit(solution)/shard_map/reduce_scatter | solution.py:72
  125.6 11.7 %copy-start.4 = (s32[1,1,80]{2,1,0:T(1,128)S(1)}, s32[1,1,80]{2,1,0:T(1,128)}, u32[]{:S(2)}) copy-start(s32[1,1,80]{2,1,0:T(1,128)} %param.13) | copy-start | bytes 964
  146.1 132.7 %reduce-scatter.5.cloned.1.call-start = ((), (), s32[]{:S(2)}) async-start(), calls=%async_computation.7 | async-start | bytes 4456448 | tf_op jit(solution)/shard_map/reduce_scatter | solution.py:58
  202.2 129.7 %all-gather.8.cloned.1.call-start = ((), (), s32[]{:S(2)}) async-start(), calls=%async_computation.11 | async-start | bytes 4456448 | tf_op jit(solution)/shard_map/all_gather | solution.py:77
  280.9 106.4 %all-gather.6.cloned.1.call-start = ((), (), s32[]{:S(2)}) async-start(), calls=%async_computation.8 | async-start | bytes 2359296 | tf_op jit(solution)/shard_map/all_gather | solution.py:61
  283.1 148.7 %reduce-scatter.11.cloned.1.call-start = ((), (), s32[]{:S(2)}) async-start(), calls=%async_computation.12 | async-start | bytes 2359296 | tf_op jit(solution)/shard_map/reduce_scatter | solution.py:79
  376.9 9.2 %copy-start.5 = (f32[256,256]{1,0:T(8,128)S(1)}, f32[256,256]{1,0:T(8,128)}, u32[]{:S(2)}) copy-start(f32[256,256]{1,0:T(8,128)} %reduce-scatter.9.cloned.1.call-done) | copy-start | bytes 786436
  376.9 9.2 %copy-start.6 = (f32[256,256]{1,0:T(8,128)S(1)}, f32[256,256]{1,0:T(8,128)}, u32[]{:S(2)}) copy-start(f32[256,256]{1,0:T(8,128)} %reduce-scatter.5.cloned.1.call-done) | copy-start | bytes 786436
  385.8 194.6 %all-reduce.3.cloned.1.call-start = ((), (), s32[]{:S(2)}) async-start(), calls=%async_computation.13 | async-start | bytes 786432 | tf_op jit(solution)/shard_map/psum | solution.py:81
  434.0 228.7 %copy-start.1 = (f32[256,256]{1,0:T(8,128)S(1)}, f32[256,256]{1,0:T(8,128)}, u32[]{:S(2)}) copy-start(f32[256,256]{1,0:T(8,128)} %param.16) | copy-start | bytes 786436
  434.1 227.0 %reduce-scatter.7.cloned.1.call-start = ((), (), s32[]{:S(2)}) async-start(), calls=%async_computation.9 | async-start | bytes 4456448 | tf_op jit(solution)/shard_map/reduce_scatter | solution.py:63
Sparse Core Ops, SparseCore 0:
  33.0 24.8 all-gather.3
  146.2 31.1 reduce-scatter.8
  202.3 76.3 reduce-scatter.4
  281.3 50.5 all-gather.7
  334.1 24.8 all-gather.5
  385.9 33.6 reduce-scatter.10
  434.2 146.1 all-reduce.2
  584.3 76.7 reduce-scatter.6
